TPU v7x, 256 devices: a whole 4x4x8 slice. The times are simulated.
256 devices in a mesh: dp: 16 (over x, y), head: 16 (over z, core).
Axes of the slice: x: 4, y: 4, z: 8, core: 2. Of those that a mesh axis runs over, the one named last changes fastest.
Arguments:
- latents: bfloat16 [2048, 512], P('dp'), may hold values from -6 to 6
- targets: bfloat16 [2048, 32768], P('dp', 'head'), may hold values from -6 to 6
- kv_weight: bfloat16 [512, 32768], P(None, 'head'), may hold values from -0.25 to 0.25
- momentum: float32 [512, 16, 2048], P(None, 'head', 'dp'), may hold values from -120 to 120
Outputs:
- momentum_out: float32 [512, 16, 2048], P(None, 'head', 'dp')
- update: float32 [512, 16, 2048], P(None, 'head', 'dp')
All inputs are finite; a program needn't handle non-finite values.
Results may differ from a plain program's by a relative error of at most 0.0003.
The roundings to bfloat16 on the way count: a program that leaves them out, or rounds other values in their place, can miss the bound.
Values may be sent and summed in bfloat16 or wider, within the bound.
A program may use at most 64 MiB of HBM per device.

v0:
```python
import math
import jax
import jax.numpy as jnp
from jax import lax
from jax.sharding import PartitionSpec as P

C = 32768
decay_rate = 0.95
linear_coef = 3.4445
square_coef = -4.775
quint_coef = 2.0315
epsilon = 1e-07
HIGHEST = lax.Precision.HIGHEST


def local(latents, targets, kv_weight, momentum):
    latent_width = momentum.shape[0]
    sub_width = momentum.shape[2]
    total_tokens = latents.shape[0] * lax.axis_size("dp")
    all_latents = lax.all_gather(latents, "dp", axis=0, tiled=True)
    my_targets = lax.all_to_all(targets, "dp", split_axis=1, concat_axis=0, tiled=True)
    start = lax.axis_index("dp") * sub_width
    my_weight = lax.dynamic_slice(kv_weight, (0, start), (latent_width, sub_width))
    residual = (
        jnp.dot(all_latents, my_weight, preferred_element_type=jnp.float32)
        - my_targets.astype(jnp.float32)
    ).astype(jnp.bfloat16)
    gradient = lax.dot_general(
        all_latents, residual, (((0,), (0,)), ((), ())), preferred_element_type=jnp.float32
    ) * (1.0 / math.sqrt(total_tokens))
    momentum_new = decay_rate * momentum.reshape(latent_width, sub_width) + gradient
    nesterov = gradient + decay_rate * momentum_new
    gram = lax.psum(
        lax.dot_general(nesterov, nesterov, (((1,), (1,)), ((), ())), precision=HIGHEST),
        ("dp", "head"),
    )
    inverse = 1.0 / (jnp.sqrt(jnp.trace(gram)) + epsilon)
    gram = gram * (inverse * inverse)
    eye = jnp.eye(latent_width, dtype=jnp.float32)
    first = (
        linear_coef * eye + square_coef * gram + quint_coef * jnp.dot(gram, gram, precision=HIGHEST)
    )
    second_gram = jnp.dot(first, jnp.dot(gram, first, precision=HIGHEST), precision=HIGHEST)
    second = (
        linear_coef * eye
        + square_coef * second_gram
        + quint_coef * jnp.dot(second_gram, second_gram, precision=HIGHEST)
    )
    iterate = jnp.dot(first, nesterov * (inverse * math.sqrt(C)), precision=HIGHEST)
    update = jnp.dot(second, iterate, precision=HIGHEST)
    return (
        momentum_new.reshape(latent_width, 1, sub_width),
        update.reshape(latent_width, 1, sub_width),
    )


def solution(mesh):
    return jax.shard_map(
        local,
        mesh=mesh,
        in_specs=(P("dp", None), P("dp", "head"), P(None, "head"), P(None, "head", "dp")),
        out_specs=(P(None, "head", "dp"), P(None, "head", "dp")),
        check_vma=False,
    )
```

profile of v0, /device:TPU:2, one launch (start us, length us, event | category | flops | bytes accessed | tf_op | source)
XLA Modules:
  0.0 346.6 jit_solution(12459691134939242747)
XLA Ops:
  7.2 0.0 copy-start
  7.2 0.0 copy-start.2
  7.2 0.0 all-gather.2.cloned.1.call-start
  7.2 0.7 all-gather.2.cloned.1.call-update
  7.9 2.0 copy.13
  10.0 7.5 %all-to-all-start = ((bf16[128,16,128]{0,2,1:T(8,128)(2,1)}), bf16[128,16,128]{0,2,1:T(8,128)(2,1)}, u32[]{:S(2)}, u32[]{:S(2)}) async-start(bf16[128,16,128]{0,2,1:T(8,128)(2,1)} %bitcast.2), calls=%async_computation | async-start | bytes 1048576 | tf_op jit(solution)/shard_map/all_to_all | solution.py:21
  17.5 0.0 all-reduce.2.cloned.1.call-start
  17.5 0.0 copy-done.2
  17.5 0.1 copy.12
  17.6 9.2 %all-to-all-done = bf16[128,16,128]{0,2,1:T(8,128)(2,1)} async-done(((bf16[128,16,128]{0,2,1:T(8,128)(2,1)}), bf16[128,16,128]{0,2,1:T(8,128)(2,1)}, u32[]{:S(2)}, u32[]{:S(2)}) %all-to-all-start) | async-done | bytes 524320 | tf_op jit(solution)/shard_map/all_to_all | solution.py:21
  26.9 1.1 convert_bitcast_fusion
  28.0 1.3 copy.14
  29.3 2.6 copy.15
  31.9 31.2 %all-gather.2.cloned.1.call-done = bf16[2048,512]{1,0:T(8,128)(2,1)} async-done(((bf16[128,512]{1,0:T(8,128)(2,1)}), bf16[2048,512]{1,0:T(8,128)(2,1)}) %all-gather.2.cloned.1.call-update) | async-done | bytes 2097168 | tf_op jit(solution)/shard_map/all_gather | solution.py:20
  63.1 0.0 copy-done
  63.1 3.7 %fusion.6 = f32[512,128]{0,1:T(8,128)S(1)} fusion(bf16[2048,512]{1,0:T(8,128)(2,1)} %all-gather.2.cloned.1.call-done, f32[2048,128]{0,1:T(8,128)} %copy.15, bf16[512,2048]{1,0:T(8,128)(2,1)S(1)} %copy-done, s32[]{:T(128)S(6)} %select_n.8), kind=kOutput, calls=%fused_computation.11 | convolution fusion | flops 537460736 | bytes 5636100 | tf_op jit(solution)/shard_map/dot_general | solution.py:28
  66.7 2.1 fusion.18
  68.8 0.0 all-reduce.2.cloned.1.call-update
  68.9 0.8 copy.16
  69.7 255.0 %all-reduce.2.cloned.1.call-done = f32[512,512]{1,0:T(8,128)} async-done(((f32[512,512]{1,0:T(8,128)}), f32[512,512]{1,0:T(8,128)}) %all-reduce.2.cloned.1.call-update) | async-done | bytes 1048592 | tf_op jit(solution)/shard_map/psum | solution.py:33
  324.7 1.9 select_reduce_fusion
  327.3 0.0 copy-start.1
  327.4 4.1 %fusion.3 = f32[512,512]{1,0:T(8,128)S(1)} fusion(f32[512,512]{1,0:T(8,128)} %all-reduce.2.cloned.1.call-done, f32[]{:T(128)S(6)} %mul.65), kind=kOutput, calls=%fused_computation.8 | convolution fusion | flops 1612709888 | bytes 2097156 | tf_op jit(solution)/shard_map/dot_general | solution.py:41
  331.4 1.0 fusion.12
  332.4 0.0 copy-done.1
  332.4 1.9 fusion.8
  334.3 1.8 fusion.23
  336.2 1.9 fusion.2
  338.1 1.7 fusion.24
  (1 shorter events, 0.0 us)
Async XLA Ops:
  7.2 55.9 %copy-start = (bf16[512,2048]{1,0:T(8,128)(2,1)S(1)}, bf16[512,2048]{1,0:T(8,128)(2,1)}, u32[]{:S(2)}) copy-start(bf16[512,2048]{1,0:T(8,128)(2,1)} %param.6) | copy-start | bytes 6291460
  7.2 10.3 %copy-start.2 = (f32[512,1,128]{2,1,0:T(1,128)S(1)}, f32[512,1,128]{2,1,0:T(1,128)}, u32[]{:S(2)}) copy-start(f32[512,1,128]{2,1,0:T(1,128)} %param.7) | copy-start | bytes 786436
  7.2 55.9 %all-gather.2.cloned.1.call-start = ((), (), s32[]{:S(2)}) async-start(), calls=%async_computation.1 | async-start | bytes 2228224 | tf_op jit(solution)/shard_map/all_gather | solution.py:20
  10.0 16.9 %all-to-all-start = ((bf16[128,16,128]{0,2,1:T(8,128)(2,1)}), bf16[128,16,128]{0,2,1:T(8,128)(2,1)}, u32[]{:S(2)}, u32[]{:S(2)}) async-start(bf16[128,16,128]{0,2,1:T(8,128)(2,1)} %bitcast.2), calls=%async_computation | async-start | bytes 1048576 | tf_op jit(solution)/shard_map/all_to_all | solution.py:21
  17.5 307.3 %all-reduce.2.cloned.1.call-start = ((), (), s32[]{:S(2)}) async-start(), calls=%async_computation.2 | async-start | bytes 2097152 | tf_op jit(solution)/shard_map/psum | solution.py:33
  327.3 5.1 %copy-start.1 = (f32[512,512]{1,0:T(8,128)S(1)}, f32[512,512]{1,0:T(8,128)}, u32[]{:S(2)}) copy-start(f32[512,512]{1,0:T(8,128)} %all-reduce.2.cloned.1.call-done) | copy-start | bytes 3145732
Sparse Core Ops, SparseCore 0:
  10.5 52.5 all-gather.1
  68.9 255.7 all-reduce.1
where the time goes:
time: 347 us
  waiting for transfers between devices  296 us (85%)
  matrix products  18.1 us (5%)
  between operations  14.9 us (4%)
  starting transfers between devices  7.55 us (2%)
  local copies, waits for them, and re-layouts  6.9 us (2%)
    psum x1, waiting for transfers between devices, local(): lax.psum(lax.dot_general(nesterov, nesterov, (((1,), (1,)), ((), ())), pr...  255 us
    all_gather x1, waiting for transfers between devices, local(): all_latents = lax.all_gather(latents, 'dp', axis=0, tiled=True)  31.2 us
    all_to_all x1, waiting for transfers between devices, local(): lax.all_to_all(targets, 'dp', split_axis=1, concat_axis=0, tiled=True)  9.24 us
    all_to_all x1, starting transfers between devices, local(): lax.all_to_all(targets, 'dp', split_axis=1, concat_axis=0, tiled=True)  7.48 us
  transfers between devices with their start and end apart: 3, of which 3 were waited for; matrix products, arithmetic and copies ran while one was open for 2% of the time, Pallas kernels for 0%

commit v1 on v0

--- a/solution.py
+++ b/solution.py
@@ -17,7 +17,21 @@
     latent_width = momentum.shape[0]
     sub_width = momentum.shape[2]
     total_tokens = latents.shape[0] * lax.axis_size("dp")
-    all_latents = lax.all_gather(latents, "dp", axis=0, tiled=True)
+    ways, here, hop = (lax.axis_size("dp"), lax.axis_index("dp"), latents.shape[0])
+    shape = [n * ways if d == 0 else n for d, n in enumerate(latents.shape)]
+    full = lax.dynamic_update_slice_in_dim(
+        jnp.zeros(shape, latents.dtype), latents, here * hop, axis=0
+    )
+    going_up = going_down = latents
+    for far in range(1, ways // 2 + 1):
+        going_up = lax.ppermute(going_up, "dp", [(d, (d + 1) % ways) for d in range(ways)])
+        full = lax.dynamic_update_slice_in_dim(full, going_up, (here - far) % ways * hop, axis=0)
+        if 2 * far < ways:
+            going_down = lax.ppermute(going_down, "dp", [(d, (d - 1) % ways) for d in range(ways)])
+            full = lax.dynamic_update_slice_in_dim(
+                full, going_down, (here + far) % ways * hop, axis=0
+            )
+    all_latents = full
     my_targets = lax.all_to_all(targets, "dp", split_axis=1, concat_axis=0, tiled=True)
     start = lax.axis_index("dp") * sub_width
     my_weight = lax.dynamic_slice(kv_weight, (0, start), (latent_width, sub_width))

time: 347 us -> 369 us (1.063)
  starting transfers between devices: 7.55 us -> 36.4 us
  waiting for transfers between devices: 296 us -> 275 us
  local copies, waits for them, and re-layouts: 6.9 us -> 18.4 us
    all_gather x1 -> x0, waiting for transfers between devices: 31.2 us -> none  [local(): all_latents = lax.all_gather(latents, 'dp', axis=0, tiled=True)]
    ppermute x0 -> x15, starting transfers between devices: none -> 29.5 us  [the longest x7 26.3 us: local(): lax.ppermute(going_down, 'dp', [(d, (d - 1) % ways) for d in range(ways)])]
    ppermute x0 -> x15, waiting for transfers between devices: none -> 14.2 us  [the longest x8 14.2 us: local(): lax.ppermute(going_up, 'dp', [(d, (d + 1) % ways) for d in range(ways)])]
    dynamic_update_slice x0 -> x16, local copies, waits for them, and re-layouts: none -> 13.3 us  [the longest x7 6.41 us: local(): lax.dynamic_update_slice_in_dim(full, going_down, (here + far) % ways * h...]
    all_to_all x1, waiting for transfers between devices: 9.24 us -> 0.01 us  [local(): lax.all_to_all(targets, 'dp', split_axis=1, concat_axis=0, tiled=True)]
    psum x1, waiting for transfers between devices: 255 us -> 261 us  [local(): lax.psum(lax.dot_general(nesterov, nesterov, (((1,), (1,)), ((), ())), pr...]
  transfers between devices with their start and end apart: 3 -> 17, of which waited for: 3 -> 6; matrix products, arithmetic and copies ran while one was open for 2% -> 5% of each run, Pallas kernels for 0% -> 0%
where the time goes in v1:
time: 369 us
  waiting for transfers between devices  275 us (75%)
  starting transfers between devices  36.4 us (10%)
  matrix products  20.4 us (6%)
  local copies, waits for them, and re-layouts  18.4 us (5%)
  between operations  15.2 us (4%)
    psum x1, waiting for transfers between devices, local(): lax.psum(lax.dot_general(nesterov, nesterov, (((1,), (1,)), ((), ())), pr...  261 us
    ppermute x7, starting transfers between devices, local(): lax.ppermute(going_down, 'dp', [(d, (d - 1) % ways) for d in range(ways)])  26.3 us
    ppermute x8, waiting for transfers between devices, local(): lax.ppermute(going_up, 'dp', [(d, (d + 1) % ways) for d in range(ways)])  14.2 us
  transfers between devices with their start and end apart: 17, of which 6 were waited for; matrix products, arithmetic and copies ran while one was open for 5% of the time, Pallas kernels for 0%

profile of v1, /device:TPU:2, one launch (start us, length us, event | category | flops | bytes accessed | tf_op | source)
XLA Modules:
  0.0 368.9 jit_solution(6573360001267978811)
XLA Ops:
  7.2 1.7 collective-permute-start
  8.8 2.6 collective-permute-start.1
  11.4 2.0 copy.13
  13.4 6.9 %all-to-all-start = ((bf16[128,16,128]{0,2,1:T(8,128)(2,1)}), bf16[128,16,128]{0,2,1:T(8,128)(2,1)S(1)}, u32[]{:S(2)}, u32[]{:S(2)}) async-start(bf16[128,16,128]{0,2,1:T(8,128)(2,1)} %bitcast.2), calls=%async_computation | async-start | bytes 1048576 | tf_op jit(solution)/shard_map/all_to_all | solution.py:35
  20.7 1.5 broadcast_in_dim.5
  22.8 1.5 collective-permute-start.2
  24.3 2.7 collective-permute-start.3
  28.3 2.2 collective-permute-done.2
  30.5 4.1 %collective-permute-start.5 = (bf16[128,512]{1,0:T(8,128)(2,1)S(1)}, bf16[128,512]{1,0:T(8,128)(2,1)}, u32[]{:S(2)}, u32[]{:S(2)}) collective-permute-start(bf16[128,512]{1,0:T(8,128)(2,1)S(1)} %collective-permute-done.3), channel_id=1, source_target_pairs={{0,240},{16,0},{32,16},{48,32},{64,48},{80,64},{96,80},{112,96},{1... | collective-permute-start | bytes 393224 | tf_op jit(solution)/shard_map/ppermute | solution.py:30
  35.9 1.6 collective-permute-done.4
  37.6 4.2 %collective-permute-start.7 = (bf16[128,512]{1,0:T(8,128)(2,1)}, bf16[128,512]{1,0:T(8,128)(2,1)}, u32[]{:S(2)}, u32[]{:S(2)}) collective-permute-start(bf16[128,512]{1,0:T(8,128)(2,1)} %collective-permute-done.5), channel_id=1, source_target_pairs={{0,240},{16,0},{32,16},{48,32},{64,48},{80,64},{96,80},{112,96},{1... | collective-permute-start | bytes 393224 | tf_op jit(solution)/shard_map/ppermute | solution.py:30
  42.5 1.6 constant_dynamic-update-slice_fusion.9
  44.1 1.1 convert_bitcast_fusion
  45.1 1.6 copy.14
  46.9 4.1 %collective-permute-start.9 = (bf16[128,512]{1,0:T(8,128)(2,1)}, bf16[128,512]{1,0:T(8,128)(2,1)S(1)}, u32[]{:S(2)}, u32[]{:S(2)}) collective-permute-start(bf16[128,512]{1,0:T(8,128)(2,1)} %collective-permute-done.7), channel_id=1, source_target_pairs={{0,240},{16,0},{32,16},{48,32},{64,48},{80,64},{96,80},{112,96},{1... | collective-permute-start | bytes 393224 | tf_op jit(solution)/shard_map/ppermute | solution.py:30
  51.0 1.6 constant_dynamic-update-slice_fusion.8
  52.5 1.6 constant_dynamic-update-slice_fusion.7
  54.1 4.1 %collective-permute-start.11 = (bf16[128,512]{1,0:T(8,128)(2,1)S(1)}, bf16[128,512]{1,0:T(8,128)(2,1)S(1)}, u32[]{:S(2)}, u32[]{:S(2)}) collective-permute-start(bf16[128,512]{1,0:T(8,128)(2,1)S(1)} %collective-permute-done.9), channel_id=1, source_target_pairs={{0,240},{16,0},{32,16},{48,32},{64,48},{80,64},{96,80},{112,96},{1... | collective-permute-start | bytes 393224 | tf_op jit(solution)/shard_map/ppermute | solution.py:30
  59.6 2.3 collective-permute-done.10
  61.9 4.4 %collective-permute-start.13 = (bf16[128,512]{1,0:T(8,128)(2,1)S(1)}, bf16[128,512]{1,0:T(8,128)(2,1)S(1)}, u32[]{:S(2)}, u32[]{:S(2)}) collective-permute-start(bf16[128,512]{1,0:T(8,128)(2,1)S(1)} %collective-permute-done.11), channel_id=1, source_target_pairs={{0,240},{16,0},{32,16},{48,32},{64,48},{80,64},{96,80},{112,96},{1... | collective-permute-start | bytes 393224 | tf_op jit(solution)/shard_map/ppermute | solution.py:30
  67.7 2.3 collective-permute-done.12
  71.3 5.7 %collective-permute-done.14 = bf16[128,512]{1,0:T(8,128)(2,1)S(1)} collective-permute-done((bf16[128,512]{1,0:T(8,128)(2,1)S(1)}, bf16[128,512]{1,0:T(8,128)(2,1)S(1)}, u32[]{:S(2)}, u32[]{:S(2)}) %collective-permute-start.14) | collective-permute-done | bytes 131104 | tf_op jit(solution)/shard_map/ppermute | solution.py:27
  77.7 5.0 %bitcast_add_fusion = (f32[512,128]{1,0:T(8,128)}, f32[512,128]{1,0:T(8,128)}) fusion(f32[512,1,128]{2,0,1:T(8,128)S(1)} %bitcast.30, bf16[2048,512]{1,0:T(8,128)(2,1)} %constant_dynamic-update-slice_fusion, f32[2048,128]{1,0:T(8,128)S(1)} %bitcast.29, bf16[512,2048]{1,0:T(8,128)(2,1)S(1)} %copy-done, s32[]{:T(128)S(6)} %select_n.117), kind=kOutput, calls=%fused_computation.18 | convolution fusion | flops 537591808 | bytes 6160388 | tf_op jit(solution)/shard_map/dot_general | solution.py:42
  82.7 3.0 fusion.15
  85.7 261.1 %all-reduce.2.cloned.1.call-done = f32[512,512]{1,0:T(8,128)} async-done(((f32[512,512]{1,0:T(8,128)}), f32[512,512]{1,0:T(8,128)}) %all-reduce.2.cloned.1.call-update) | async-done | bytes 1048592 | tf_op jit(solution)/shard_map/psum | solution.py:47
  346.9 2.0 select_reduce_fusion
  349.6 4.1 %fusion.2 = f32[512,512]{1,0:T(8,128)S(1)} fusion(f32[512,512]{1,0:T(8,128)} %all-reduce.2.cloned.1.call-done, f32[]{:T(128)S(6)} %mul.122), kind=kOutput, calls=%fused_computation.7 | convolution fusion | flops 1612709888 | bytes 2097156 | tf_op jit(solution)/shard_map/dot_general | solution.py:55
  353.7 1.0 fusion.10
  354.7 1.9 fusion.6
  356.6 1.8 fusion.22
  358.4 1.9 fusion.1
  360.3 1.7 fusion.23
  (42 shorter events, 8.8 us)
Async XLA Ops:
  7.2 70.5 %copy-start = (bf16[512,2048]{1,0:T(8,128)(2,1)S(1)}, bf16[512,2048]{1,0:T(8,128)(2,1)}, u32[]{:S(2)}) copy-start(bf16[512,2048]{1,0:T(8,128)(2,1)} %param.6) | copy-start | bytes 6291460
  7.2 15.0 %copy-start.4 = (bf16[128,512]{1,0:T(8,128)(2,1)S(1)}, bf16[128,512]{1,0:T(8,128)(2,1)}, u32[]{:S(2)}) copy-start(bf16[128,512]{1,0:T(8,128)(2,1)} %param.4) | copy-start | bytes 393220
  7.2 15.6 %collective-permute-start = (bf16[128,512]{1,0:T(8,128)(2,1)}, bf16[128,512]{1,0:T(8,128)(2,1)S(1)}, u32[]{:S(2)}, u32[]{:S(2)}) collective-permute-start(bf16[128,512]{1,0:T(8,128)(2,1)} %param.4), channel_id=1, source_target_pairs={{0,16},{16,32},{32,48},{48,64},{64,80},{80,96},{96,112},{112,128},... | collective-permute-start | bytes 393224 | tf_op jit(solution)/shard_map/ppermute | solution.py:27
  8.8 15.4 %collective-permute-start.1 = (bf16[128,512]{1,0:T(8,128)(2,1)}, bf16[128,512]{1,0:T(8,128)(2,1)S(1)}, u32[]{:S(2)}, u32[]{:S(2)}) collective-permute-start(bf16[128,512]{1,0:T(8,128)(2,1)} %param.4), channel_id=1, source_target_pairs={{0,240},{16,0},{32,16},{48,32},{64,48},{80,64},{96,80},{112,96},{1... | collective-permute-start | bytes 393224 | tf_op jit(solution)/shard_map/ppermute | solution.py:30
  13.4 30.6 %all-to-all-start = ((bf16[128,16,128]{0,2,1:T(8,128)(2,1)}), bf16[128,16,128]{0,2,1:T(8,128)(2,1)S(1)}, u32[]{:S(2)}, u32[]{:S(2)}) async-start(bf16[128,16,128]{0,2,1:T(8,128)(2,1)} %bitcast.2), calls=%async_computation | async-start | bytes 1048576 | tf_op jit(solution)/shard_map/all_to_all | solution.py:35
  20.3 326.6 %all-reduce.2.cloned.1.call-start = ((), (), s32[]{:S(2)}) async-start(), calls=%async_computation.1 | async-start | bytes 2097152 | tf_op jit(solution)/shard_map/psum | solution.py:47
  22.8 7.7 %collective-permute-start.2 = (bf16[128,512]{1,0:T(8,128)(2,1)S(1)}, bf16[128,512]{1,0:T(8,128)(2,1)S(1)}, u32[]{:S(2)}, u32[]{:S(2)}) collective-permute-start(bf16[128,512]{1,0:T(8,128)(2,1)S(1)} %collective-permute-done), channel_id=1, source_target_pairs={{0,16},{16,32},{32,48},{48,64},{64,80},{80,96},{96,112},{112,128},... | collective-permute-start | bytes 393224 | tf_op jit(solution)/shard_map/ppermute | solution.py:27
  24.3 6.2 %collective-permute-start.3 = (bf16[128,512]{1,0:T(8,128)(2,1)S(1)}, bf16[128,512]{1,0:T(8,128)(2,1)S(1)}, u32[]{:S(2)}, u32[]{:S(2)}) collective-permute-start(bf16[128,512]{1,0:T(8,128)(2,1)S(1)} %collective-permute-done.1), channel_id=1, source_target_pairs={{0,240},{16,0},{32,16},{48,32},{64,48},{80,64},{96,80},{112,96},{1... | collective-permute-start | bytes 393224 | tf_op jit(solution)/shard_map/ppermute | solution.py:30
  30.5 7.1 %collective-permute-start.4 = (bf16[128,512]{1,0:T(8,128)(2,1)S(1)}, bf16[128,512]{1,0:T(8,128)(2,1)S(1)}, u32[]{:S(2)}, u32[]{:S(2)}) collective-permute-start(bf16[128,512]{1,0:T(8,128)(2,1)S(1)} %collective-permute-done.2), channel_id=1, source_target_pairs={{0,16},{16,32},{32,48},{48,64},{64,80},{80,96},{96,112},{112,128},... | collective-permute-start | bytes 393224 | tf_op jit(solution)/shard_map/ppermute | solution.py:27
  30.5 7.1 %collective-permute-start.5 = (bf16[128,512]{1,0:T(8,128)(2,1)S(1)}, bf16[128,512]{1,0:T(8,128)(2,1)}, u32[]{:S(2)}, u32[]{:S(2)}) collective-permute-start(bf16[128,512]{1,0:T(8,128)(2,1)S(1)} %collective-permute-done.3), channel_id=1, source_target_pairs={{0,240},{16,0},{32,16},{48,32},{64,48},{80,64},{96,80},{112,96},{1... | collective-permute-start | bytes 393224 | tf_op jit(solution)/shard_map/ppermute | solution.py:30
  37.6 9.2 %collective-permute-start.6 = (bf16[128,512]{1,0:T(8,128)(2,1)S(1)}, bf16[128,512]{1,0:T(8,128)(2,1)}, u32[]{:S(2)}, u32[]{:S(2)}) collective-permute-start(bf16[128,512]{1,0:T(8,128)(2,1)S(1)} %collective-permute-done.4), channel_id=1, source_target_pairs={{0,16},{16,32},{32,48},{48,64},{64,80},{80,96},{96,112},{112,128},... | collective-permute-start | bytes 393224 | tf_op jit(solution)/shard_map/ppermute | solution.py:27
  37.6 9.3 %collective-permute-start.7 = (bf16[128,512]{1,0:T(8,128)(2,1)}, bf16[128,512]{1,0:T(8,128)(2,1)}, u32[]{:S(2)}, u32[]{:S(2)}) collective-permute-start(bf16[128,512]{1,0:T(8,128)(2,1)} %collective-permute-done.5), channel_id=1, source_target_pairs={{0,240},{16,0},{32,16},{48,32},{64,48},{80,64},{96,80},{112,96},{1... | collective-permute-start | bytes 393224 | tf_op jit(solution)/shard_map/ppermute | solution.py:30
  45.1 32.6 %copy-start.2 = (f32[512,1,128]{2,1,0:T(1,128)S(1)}, f32[512,1,128]{2,1,0:T(1,128)}, u32[]{:S(2)}) copy-start(f32[512,1,128]{2,1,0:T(1,128)} %param.7) | copy-start | bytes 786436
  46.8 7.4 %collective-permute-start.8 = (bf16[128,512]{1,0:T(8,128)(2,1)}, bf16[128,512]{1,0:T(8,128)(2,1)S(1)}, u32[]{:S(2)}, u32[]{:S(2)}) collective-permute-start(bf16[128,512]{1,0:T(8,128)(2,1)} %collective-permute-done.6), channel_id=1, source_target_pairs={{0,16},{16,32},{32,48},{48,64},{64,80},{80,96},{96,112},{112,128},... | collective-permute-start | bytes 393224 | tf_op jit(solution)/shard_map/ppermute | solution.py:27
  46.9 7.3 %collective-permute-start.9 = (bf16[128,512]{1,0:T(8,128)(2,1)}, bf16[128,512]{1,0:T(8,128)(2,1)S(1)}, u32[]{:S(2)}, u32[]{:S(2)}) collective-permute-start(bf16[128,512]{1,0:T(8,128)(2,1)} %collective-permute-done.7), channel_id=1, source_target_pairs={{0,240},{16,0},{32,16},{48,32},{64,48},{80,64},{96,80},{112,96},{1... | collective-permute-start | bytes 393224 | tf_op jit(solution)/shard_map/ppermute | solution.py:30
  54.1 7.8 %collective-permute-start.10 = (bf16[128,512]{1,0:T(8,128)(2,1)S(1)}, bf16[128,512]{1,0:T(8,128)(2,1)S(1)}, u32[]{:S(2)}, u32[]{:S(2)}) collective-permute-start(bf16[128,512]{1,0:T(8,128)(2,1)S(1)} %collective-permute-done.8), channel_id=1, source_target_pairs={{0,16},{16,32},{32,48},{48,64},{64,80},{80,96},{96,112},{112,128},... | collective-permute-start | bytes 393224 | tf_op jit(solution)/shard_map/ppermute | solution.py:27
  54.1 7.8 %collective-permute-start.11 = (bf16[128,512]{1,0:T(8,128)(2,1)S(1)}, bf16[128,512]{1,0:T(8,128)(2,1)S(1)}, u32[]{:S(2)}, u32[]{:S(2)}) collective-permute-start(bf16[128,512]{1,0:T(8,128)(2,1)S(1)} %collective-permute-done.9), channel_id=1, source_target_pairs={{0,240},{16,0},{32,16},{48,32},{64,48},{80,64},{96,80},{112,96},{1... | collective-permute-start | bytes 393224 | tf_op jit(solution)/shard_map/ppermute | solution.py:30
  61.9 8.0 %collective-permute-start.12 = (bf16[128,512]{1,0:T(8,128)(2,1)S(1)}, bf16[128,512]{1,0:T(8,128)(2,1)S(1)}, u32[]{:S(2)}, u32[]{:S(2)}) collective-permute-start(bf16[128,512]{1,0:T(8,128)(2,1)S(1)} %collective-permute-done.10), channel_id=1, source_target_pairs={{0,16},{16,32},{32,48},{48,64},{64,80},{80,96},{96,112},{112,128},... | collective-permute-start | bytes 393224 | tf_op jit(solution)/shard_map/ppermute | solution.py:27
  61.9 8.7 %collective-permute-start.13 = (bf16[128,512]{1,0:T(8,128)(2,1)S(1)}, bf16[128,512]{1,0:T(8,128)(2,1)S(1)}, u32[]{:S(2)}, u32[]{:S(2)}) collective-permute-start(bf16[128,512]{1,0:T(8,128)(2,1)S(1)} %collective-permute-done.11), channel_id=1, source_target_pairs={{0,240},{16,0},{32,16},{48,32},{64,48},{80,64},{96,80},{112,96},{1... | collective-permute-start | bytes 393224 | tf_op jit(solution)/shard_map/ppermute | solution.py:30
  69.9 7.1 %collective-permute-start.14 = (bf16[128,512]{1,0:T(8,128)(2,1)S(1)}, bf16[128,512]{1,0:T(8,128)(2,1)S(1)}, u32[]{:S(2)}, u32[]{:S(2)}) collective-permute-start(bf16[128,512]{1,0:T(8,128)(2,1)S(1)} %collective-permute-done.12), channel_id=1, source_target_pairs={{0,16},{16,32},{32,48},{48,64},{64,80},{80,96},{96,112},{112,128},... | collective-permute-start | bytes 393224 | tf_op jit(solution)/shard_map/ppermute | solution.py:27
  85.7 268.0 %copy-start.3 = (f32[512,128]{1,0:T(8,128)S(1)}, f32[512,128]{1,0:T(8,128)}, u32[]{:S(2)}) copy-start(f32[512,128]{1,0:T(8,128)} %get-tuple-element.9) | copy-start | bytes 786436
  349.6 5.1 %copy-start.1 = (f32[512,512]{1,0:T(8,128)S(1)}, f32[512,512]{1,0:T(8,128)}, u32[]{:S(2)}) copy-start(f32[512,512]{1,0:T(8,128)} %all-reduce.2.cloned.1.call-done) | copy-start | bytes 3145732
Sparse Core Ops, SparseCore 0:
  85.9 260.9 all-reduce.1
